TPU v7x, 32 devices: a whole 2x2x4 slice. The times are simulated.
32 devices in a mesh: member: 2 (over x), gx: 16 (over z, y, core).
Axes of the slice: x: 2, y: 2, z: 4, core: 2. Of those that a mesh axis runs over, the one named last changes fastest.
Arguments:
- electric: float32 [3, 64, 256, 128], P(None, 'gx'), may hold values from -6 to 6
- magnetic: float32 [3, 64, 256, 128], P(None, 'gx'), may hold values from -6 to 6
- material: int32 [128, 256, 128], P(('member', 'gx')), parts along dimension 0, may hold values from 0 to 3, as said below
- permittivity: float32 [4], replicated, may hold values from 1 to 4
- pole_frequency: float32 [2], replicated, may hold values from 0.3 to 1.2
- pole_damping: float32 [2], replicated, may hold values from 0.05 to 1
- pole_strength: float32 [2], replicated, may hold values from 0.3 to 2
- frequencies: float32 [8], replicated, may hold values from 0.2 to 2
- plane_depth: int32 [4], replicated, may hold values from 1 to 126
- mode_fields: float32 [4, 4, 64, 256], P(None, None, 'gx'), may hold values from -40 to 40
Outputs:
- electric_final: float32 [3, 128, 256, 128], P(None, ('member', 'gx')), parts along dimension 1
- magnetic_final: float32 [3, 128, 256, 128], P(None, ('member', 'gx')), parts along dimension 1
- monitors: float32 [2, 4, 8, 4, 128, 256], P(None, None, None, None, ('member', 'gx')), parts along dimension 4
- intersection: float32 [4, 4, 8], P('member'), parts along dimension 0
There are 2 independent parts, one for each index of `member`. A program takes and returns all parts, laid end to end along the dimension named above; an argument that names none is the same for every part. Nothing has to cross between parts.
Inputs may be any that keep to these rules, and one draw needn't show every extreme that they name: Each 16-layer thickness profile stacks layers along the first dimension, each of one material, with a lateral lattice of material 0 cells in some layers; materials 2 and above are dispersive.
All inputs are finite; a program needn't handle non-finite values.
Results may differ from a plain program's by a relative error of at most 0.0003.
Values sent between devices are 32-bit elements; how exact they have to be, the bound alone decides.
A program may use at most 64 MiB of HBM per device.

v0:
```python
import math

import jax
import jax.numpy as jnp
from jax import lax
from jax.sharding import PartitionSpec as P

STEPS = 6


DT = 0.5


def shifted(value, axis, steps):
    count = lax.axis_size(axis)
    first, last = (max(0, -steps), min(count, count - steps))
    return lax.ppermute(value, axis, [(source, source + steps) for source in range(first, last)])


def zero_rim(field, direction):
    return jnp.zeros_like(lax.slice_in_dim(field, 0, 1, axis=direction))


def diff_ahead(field, direction, beyond):
    remainder = lax.slice_in_dim(field, 1, field.shape[direction], axis=direction)
    return jnp.concatenate([remainder, beyond], axis=direction) - field


def diff_behind(field, direction, preceding):
    remainder = lax.slice_in_dim(field, 0, field.shape[direction] - 1, axis=direction)
    return field - jnp.concatenate([preceding, remainder], axis=direction)


def ahead_open(field, direction):
    return diff_ahead(field, direction, zero_rim(field, direction))


def behind_open(field, direction):
    return diff_behind(field, direction, zero_rim(field, direction))


def curl_e(e_field, upper):
    first = ahead_open(e_field[2], 1) - ahead_open(e_field[1], 2)
    second = ahead_open(e_field[0], 2) - diff_ahead(e_field[2], 0, upper[1])
    third = diff_ahead(e_field[1], 0, upper[0]) - ahead_open(e_field[0], 1)
    return jnp.stack([first, second, third])


def curl_h(h_field, lower):
    first = behind_open(h_field[2], 1) - behind_open(h_field[1], 2)
    second = behind_open(h_field[0], 2) - diff_behind(h_field[2], 0, lower[1])
    third = diff_behind(h_field[1], 0, lower[0]) - behind_open(h_field[0], 1)
    return jnp.stack([first, second, third])


def coefficients(material, permittivity, pole_frequency, pole_damping, pole_strength):
    eps_cell = jnp.zeros(material.shape, jnp.float32)
    for kind_index in range(permittivity.shape[0]):
        eps_cell = eps_cell + jnp.where(material == kind_index, permittivity[kind_index], 0.0)
    damping = jnp.zeros(material.shape, jnp.float32)
    square = jnp.zeros(material.shape, jnp.float32)
    driving = jnp.zeros(material.shape, jnp.float32)
    offset = permittivity.shape[0] - pole_frequency.shape[0]
    for pole_index in range(pole_frequency.shape[0]):
        chosen = material == pole_index + offset
        freq_sq = pole_frequency[pole_index] * pole_frequency[pole_index]
        damping = damping + jnp.where(chosen, pole_damping[pole_index], 0.0)
        square = square + jnp.where(chosen, freq_sq, 0.0)
        driving = driving + jnp.where(chosen, pole_strength[pole_index] * freq_sq, 0.0)
    divisor = 1.0 + 0.5 * DT * damping
    retain = (1.0 - 0.5 * DT * damping) / divisor
    pulling = DT * driving / divisor
    spring = DT * square / divisor
    step_e = DT / eps_cell
    return (retain, pulling, spring, step_e)


def record(monitors, e_field, h_field, select, frequencies, step):
    plane_e = jnp.einsum("cxyz,zm->cmxy", e_field[:2], select, precision=lax.Precision.HIGHEST)
    plane_h = jnp.einsum("cxyz,zm->cmxy", h_field[:2], select, precision=lax.Precision.HIGHEST)
    planes = jnp.concatenate([plane_e, plane_h], axis=0)
    phase_e = (step + 1.0) * DT * frequencies
    phase_h = (step + 0.5) * DT * frequencies
    cosines = jnp.stack([jnp.cos(phase_e), jnp.cos(phase_e), jnp.cos(phase_h), jnp.cos(phase_h)])
    sine_part = -jnp.stack([jnp.sin(phase_e), jnp.sin(phase_e), jnp.sin(phase_h), jnp.sin(phase_h)])
    rotation = jnp.stack([cosines, sine_part])
    return monitors + rotation[:, :, :, None, None, None] * planes[None, :, None, :, :, :]


def project(monitors, mode_fields, scale):
    pairing = jnp.stack([mode_fields[3], -mode_fields[2], -mode_fields[1], mode_fields[0]])
    return scale * jnp.einsum(
        "rcfmxy,cmxy->rmf", monitors, pairing, precision=lax.Precision.HIGHEST
    )


def pole_update(current, polarized, e_field, curl_field, retain, pulling, spring, step_e):
    current = retain * current + pulling * e_field - spring * polarized
    polarized = polarized + DT * current
    e_field = e_field + step_e * (curl_field - current)
    return (current, polarized, e_field)


def on_device(
    electric,
    magnetic,
    material,
    permittivity,
    pole_frequency,
    pole_damping,
    pole_strength,
    frequencies,
    plane_depth,
    mode_fields,
):
    retain, pulling, spring, step_e = coefficients(
        material, permittivity, pole_frequency, pole_damping, pole_strength
    )
    slab_cells = electric.shape[1]
    width_y = electric.shape[2]
    depth_z = electric.shape[3]
    select = (jnp.arange(depth_z)[:, None] == plane_depth[None, :]).astype(jnp.float32)
    current = jnp.zeros_like(electric)
    polarized = jnp.zeros_like(electric)
    monitors = jnp.zeros(
        (2, 4, frequencies.shape[0], plane_depth.shape[0], slab_cells, width_y), jnp.float32
    )
    for step in range(STEPS):
        upper = shifted(electric[1:3, :1], "gx", -1)
        magnetic = magnetic - DT * curl_e(electric, upper)
        lower = shifted(magnetic[1:3, -1:], "gx", 1)
        curl_field = curl_h(magnetic, lower)
        current, polarized, electric = pole_update(
            current, polarized, electric, curl_field, retain, pulling, spring, step_e
        )
        monitors = record(monitors, electric, magnetic, select, frequencies, step)
    scale = 1.0 / math.sqrt(4.0 * slab_cells * lax.axis_size("gx") * width_y)
    partial_value = project(monitors, mode_fields, scale)
    intersection = lax.psum(partial_value, "gx")
    return (electric, magnetic, monitors, intersection)


def solution(mesh):
    in_specs = (
        P(None, "gx", None, None),
        P(None, "gx", None, None),
        P(("member", "gx"), None, None),
        P(),
        P(),
        P(),
        P(),
        P(),
        P(),
        P(None, None, "gx", None),
    )
    out_specs = (
        P(None, ("member", "gx"), None, None),
        P(None, ("member", "gx"), None, None),
        P(None, None, None, None, ("member", "gx"), None),
        P("member", None, None),
    )
    return jax.shard_map(
        on_device, mesh=mesh, in_specs=in_specs, out_specs=out_specs, check_vma=False
    )
```

profile of v0, /device:TPU:0, one launch (start us, length us, event | category | flops | bytes accessed | tf_op | source)
XLA Modules:
  0.0 158.4 jit_solution(6075497116907819001)
XLA Ops:
  0.6 1.0 slice.656
  1.7 1.4 collective-permute-start
  3.1 1.5 slice_bitcast_fusion.35
  4.6 0.6 fusion.102
  7.8 0.6 fusion.103
  8.4 0.6 fusion.101
  9.0 0.7 fusion.100
  11.3 1.6 subtract_divide_fusion
  13.0 4.4 %broadcast_multiply_fusion.2 = (f32[4,256,128]{2,1,0:T(8,128)S(1)}, f32[4,256,128]{2,1,0:T(8,128)S(1)}, f32[4,256,128]{2,1,0:T(8,128)S(1)}, f32[4,256,128]{2,1,0:T(8,128)S(1)}, f32[4,256,128]{2,1,0:T(8,128)S(1)}) fusion(pred[4,256,128]{2,1,0:T(8,128)(4,1)S(1)} %get-tuple-element.10, f32[]{:T(128)} %bitcast.25, ...), kind=kLoop, calls=%fused_computation.218 | loop fusion | flops 3932160 | bytes 3407912 | tf_op jit(solution)/shard_map/mul | solution.py:98
  17.9 1.0 copy-done
  19.3 1.0 copy-done.1
  20.7 3.0 %collective-permute-start.1 = (f32[2,1,256,128]{3,2,1,0:T(8,128)S(1)}, f32[2,1,256,128]{3,2,1,0:T(8,128)S(1)}, u32[]{:S(2)}, u32[]{:S(2)}) collective-permute-start(f32[2,1,256,128]{3,2,1,0:T(8,128)S(1)} %slice.850), channel_id=1, source_target_pairs={{0,1},{1,2},{2,3},{3,4},{4,5},{5,6},{6,7},{7,8},{8,9},{9,10},{10,1... | collective-permute-start | bytes 786440 | tf_op jit(solution)/shard_map/ppermute | solution.py:17
  24.9 0.7 subtract_bitcast_fusion.10
  26.7 1.3 collective-permute-start.2
  28.6 5.8 %collective-permute-done.2 = f32[2,1,256,128]{3,2,1,0:T(8,128)S(1)} collective-permute-done((f32[2,1,256,128]{3,2,1,0:T(8,128)S(1)}, f32[2,1,256,128]{3,2,1,0:T(8,128)S(1)}, u32[]{:S(2)}, u32[]{:S(2)}) %collective-permute-start.2) | collective-permute-done | bytes 262176 | tf_op jit(solution)/shard_map/ppermute | solution.py:17
  35.2 7.4 %collective-permute-start.3 = (f32[2,1,256,128]{3,2,1,0:T(8,128)S(1)}, f32[2,1,256,128]{3,2,1,0:T(8,128)S(1)}, u32[]{:S(2)}, u32[]{:S(2)}) collective-permute-start(f32[2,1,256,128]{3,2,1,0:T(8,128)S(1)} %slice.874), channel_id=1, source_target_pairs={{0,1},{1,2},{2,3},{3,4},{4,5},{5,6},{6,7},{7,8},{8,9},{9,10},{10,1... | collective-permute-start | bytes 786440 | tf_op jit(solution)/shard_map/ppermute | solution.py:17
  43.8 0.7 subtract_bitcast_fusion.8
  44.5 0.8 fusion.5
  46.0 1.3 collective-permute-start.4
  47.9 3.2 %collective-permute-done.4 = f32[2,1,256,128]{3,2,1,0:T(8,128)S(1)} collective-permute-done((f32[2,1,256,128]{3,2,1,0:T(8,128)S(1)}, f32[2,1,256,128]{3,2,1,0:T(8,128)S(1)}, u32[]{:S(2)}, u32[]{:S(2)}) %collective-permute-start.4) | collective-permute-done | bytes 262176 | tf_op jit(solution)/shard_map/ppermute | solution.py:17
  52.1 7.6 %collective-permute-start.5 = (f32[2,1,256,128]{3,2,1,0:T(8,128)S(1)}, f32[2,1,256,128]{3,2,1,0:T(8,128)S(1)}, u32[]{:S(2)}, u32[]{:S(2)}) collective-permute-start(f32[2,1,256,128]{3,2,1,0:T(8,128)S(1)} %slice.898), channel_id=1, source_target_pairs={{0,1},{1,2},{2,3},{3,4},{4,5},{5,6},{6,7},{7,8},{8,9},{9,10},{10,1... | collective-permute-start | bytes 786440 | tf_op jit(solution)/shard_map/ppermute | solution.py:17
  60.7 0.7 subtract_bitcast_fusion.6
  61.4 1.3 fusion.8
  63.4 1.3 collective-permute-start.6
  65.3 3.2 %collective-permute-done.6 = f32[2,1,256,128]{3,2,1,0:T(8,128)S(1)} collective-permute-done((f32[2,1,256,128]{3,2,1,0:T(8,128)S(1)}, f32[2,1,256,128]{3,2,1,0:T(8,128)S(1)}, u32[]{:S(2)}, u32[]{:S(2)}) %collective-permute-start.6) | collective-permute-done | bytes 262176 | tf_op jit(solution)/shard_map/ppermute | solution.py:17
  68.7 0.6 fusion.9
  69.5 7.4 %collective-permute-start.7 = (f32[2,1,256,128]{3,2,1,0:T(8,128)S(1)}, f32[2,1,256,128]{3,2,1,0:T(8,128)S(1)}, u32[]{:S(2)}, u32[]{:S(2)}) collective-permute-start(f32[2,1,256,128]{3,2,1,0:T(8,128)S(1)} %slice.922), channel_id=1, source_target_pairs={{0,1},{1,2},{2,3},{3,4},{4,5},{5,6},{6,7},{7,8},{8,9},{9,10},{10,1... | collective-permute-start | bytes 786440 | tf_op jit(solution)/shard_map/ppermute | solution.py:17
  78.1 0.7 subtract_bitcast_fusion.4
  78.8 1.2 fusion.11
  80.0 0.6 convolution_bitcast_fusion.5
  80.7 1.3 collective-permute-start.8
  82.6 3.2 %collective-permute-done.8 = f32[2,1,256,128]{3,2,1,0:T(8,128)S(1)} collective-permute-done((f32[2,1,256,128]{3,2,1,0:T(8,128)S(1)}, f32[2,1,256,128]{3,2,1,0:T(8,128)S(1)}, u32[]{:S(2)}, u32[]{:S(2)}) %collective-permute-start.8) | collective-permute-done | bytes 262176 | tf_op jit(solution)/shard_map/ppermute | solution.py:17
  86.2 0.6 fusion.12
  87.0 7.9 %collective-permute-start.9 = (f32[2,1,256,128]{3,2,1,0:T(8,128)S(1)}, f32[2,1,256,128]{3,2,1,0:T(8,128)S(1)}, u32[]{:S(2)}, u32[]{:S(2)}) collective-permute-start(f32[2,1,256,128]{3,2,1,0:T(8,128)S(1)} %slice.946), channel_id=1, source_target_pairs={{0,1},{1,2},{2,3},{3,4},{4,5},{5,6},{6,7},{7,8},{8,9},{9,10},{10,1... | collective-permute-start | bytes 786440 | tf_op jit(solution)/shard_map/ppermute | solution.py:17
  94.9 0.6 convolution_bitcast_fusion.2
  96.1 0.7 subtract_bitcast_fusion.2
  96.8 1.0 fusion.14
  98.5 1.5 collective-permute-start.10
  100.6 3.0 %collective-permute-done.10 = f32[2,1,256,128]{3,2,1,0:T(8,128)S(1)} collective-permute-done((f32[2,1,256,128]{3,2,1,0:T(8,128)S(1)}, f32[2,1,256,128]{3,2,1,0:T(8,128)S(1)}, u32[]{:S(2)}, u32[]{:S(2)}) %collective-permute-start.10) | collective-permute-done | bytes 262176 | tf_op jit(solution)/shard_map/ppermute | solution.py:17
  103.9 0.8 fusion.15
  104.8 8.3 %collective-permute-start.11 = (f32[2,1,256,128]{3,2,1,0:T(8,128)S(1)}, f32[2,1,256,128]{3,2,1,0:T(8,128)S(1)}, u32[]{:S(2)}, u32[]{:S(2)}) collective-permute-start(f32[2,1,256,128]{3,2,1,0:T(8,128)S(1)} %slice.970), channel_id=1, source_target_pairs={{0,1},{1,2},{2,3},{3,4},{4,5},{5,6},{6,7},{7,8},{8,9},{9,10},{10,1... | collective-permute-start | bytes 786440 | tf_op jit(solution)/shard_map/ppermute | solution.py:17
  113.1 0.6 convolution_bitcast_fusion
  114.3 0.7 subtract_bitcast_fusion
  115.0 1.4 fusion.17
  116.4 0.6 convolution_bitcast_fusion.1
  117.0 1.1 multiply_add_fusion
  118.2 7.0 %fusion.32 = f32[4,1,2,8,1,1]{3,1,5,4,2,0:T(1,128)S(1)} fusion(f32[2,4,8,4,4,256]{5,4,3,2,1,0:T(4,128)S(1)} %multiply_add_fusion, f32[4,4,4,256,1,1]{3,2,1,0,4,5:T(4,128)S(1)} %maximum_bitcast_fusion), kind=kOutput, calls=%fused_computation.61 | convolution fusion | flops 3145728 | bytes 1114368 | tf_op jit(solution)/shard_map/rcfmxy,cmxy->rmf/dot_general | solution.py:92
  125.2 33.2 %psum.7 = f32[2,4,8]{2,1,0:T(4,128)} all-reduce(f32[2,4,8]{2,1,0:T(4,128)S(1)} %fusion.84), channel_id=1, replica_groups=mesh['member'=2,'gx'=16] {'gx'}, use_global_device_ids=true, to_apply=%region_0.1 | all-reduce | flops 64 | bytes 512 | tf_op jit(solution)/shard_map/psum | solution.py:139
  (147 shorter events, 16.3 us)
Async XLA Ops:
  1.6 3.0 %copy-start.9 = (f32[2]{0:T(128)S(1)}, f32[2]{0:T(128)}, u32[]{:S(2)}) copy-start(f32[2]{0:T(128)} %param.14) | copy-start | bytes 28
  1.6 6.2 %copy-start.10 = (f32[2]{0:T(128)S(1)}, f32[2]{0:T(128)}, u32[]{:S(2)}) copy-start(f32[2]{0:T(128)} %param.15) | copy-start | bytes 28
  1.6 6.7 %copy-start.11 = (f32[2]{0:T(128)S(1)}, f32[2]{0:T(128)}, u32[]{:S(2)}) copy-start(f32[2]{0:T(128)} %param.16) | copy-start | bytes 28
  1.6 7.3 %copy-start.8 = (f32[4]{0:T(128)S(1)}, f32[4]{0:T(128)}, u32[]{:S(2)}) copy-start(f32[4]{0:T(128)} %param.13) | copy-start | bytes 52
  1.7 8.0 %copy-start.12 = (f32[8]{0:T(128)S(1)}, f32[8]{0:T(128)}, u32[]{:S(2)}) copy-start(f32[8]{0:T(128)} %param.17) | copy-start | bytes 100
  1.7 8.2 %copy-start.7 = (f32[4,4,4,256]{3,2,1,0:T(4,128)S(1)}, f32[4,4,4,256]{3,2,1,0:T(4,128)}, u32[]{:S(2)}) copy-start(f32[4,4,4,256]{3,2,1,0:T(4,128)} %param.19) | copy-start | bytes 196612
  1.7 9.7 %copy-start.5 = (s32[4,256,128]{2,1,0:T(8,128)S(1)}, s32[4,256,128]{2,1,0:T(8,128)}, u32[]{:S(2)}) copy-start(s32[4,256,128]{2,1,0:T(8,128)} %param.12) | copy-start | bytes 1572868
  1.7 17.2 %collective-permute-start = (f32[2,1,256,128]{3,2,1,0:T(8,128)S(1)}, f32[2,1,256,128]{3,2,1,0:T(8,128)S(1)}, u32[]{:S(2)}, u32[]{:S(2)}) collective-permute-start(f32[2,1,256,128]{3,2,1,0:T(8,128)S(1)} %slice.656), channel_id=1, source_target_pairs={{1,0},{2,1},{3,2},{4,3},{5,4},{6,5},{7,6},{8,7},{9,8},{10,9},{11,1... | collective-permute-start | bytes 786440 | tf_op jit(solution)/shard_map/ppermute | solution.py:17
  17.4 1.4 copy-start
  18.9 1.4 copy-start.1
  20.6 3.2 %copy-start.6 = (s32[4]{0:T(128)S(1)}, s32[4]{0:T(128)}, u32[]{:S(2)}) copy-start(s32[4]{0:T(128)} %param.18) | copy-start | bytes 52
  20.7 4.2 %collective-permute-start.1 = (f32[2,1,256,128]{3,2,1,0:T(8,128)S(1)}, f32[2,1,256,128]{3,2,1,0:T(8,128)S(1)}, u32[]{:S(2)}, u32[]{:S(2)}) collective-permute-start(f32[2,1,256,128]{3,2,1,0:T(8,128)S(1)} %slice.850), channel_id=1, source_target_pairs={{0,1},{1,2},{2,3},{3,4},{4,5},{5,6},{6,7},{7,8},{8,9},{9,10},{10,1... | collective-permute-start | bytes 786440 | tf_op jit(solution)/shard_map/ppermute | solution.py:17
  26.7 7.7 %collective-permute-start.2 = (f32[2,1,256,128]{3,2,1,0:T(8,128)S(1)}, f32[2,1,256,128]{3,2,1,0:T(8,128)S(1)}, u32[]{:S(2)}, u32[]{:S(2)}) collective-permute-start(f32[2,1,256,128]{3,2,1,0:T(8,128)S(1)} %slice.863), channel_id=1, source_target_pairs={{1,0},{2,1},{3,2},{4,3},{5,4},{6,5},{7,6},{8,7},{9,8},{10,9},{11,1... | collective-permute-start | bytes 786440 | tf_op jit(solution)/shard_map/ppermute | solution.py:17
  35.2 8.6 %collective-permute-start.3 = (f32[2,1,256,128]{3,2,1,0:T(8,128)S(1)}, f32[2,1,256,128]{3,2,1,0:T(8,128)S(1)}, u32[]{:S(2)}, u32[]{:S(2)}) collective-permute-start(f32[2,1,256,128]{3,2,1,0:T(8,128)S(1)} %slice.874), channel_id=1, source_target_pairs={{0,1},{1,2},{2,3},{3,4},{4,5},{5,6},{6,7},{7,8},{8,9},{9,10},{10,1... | collective-permute-start | bytes 786440 | tf_op jit(solution)/shard_map/ppermute | solution.py:17
  46.0 5.1 %collective-permute-start.4 = (f32[2,1,256,128]{3,2,1,0:T(8,128)S(1)}, f32[2,1,256,128]{3,2,1,0:T(8,128)S(1)}, u32[]{:S(2)}, u32[]{:S(2)}) collective-permute-start(f32[2,1,256,128]{3,2,1,0:T(8,128)S(1)} %slice.887), channel_id=1, source_target_pairs={{1,0},{2,1},{3,2},{4,3},{5,4},{6,5},{7,6},{8,7},{9,8},{10,9},{11,1... | collective-permute-start | bytes 786440 | tf_op jit(solution)/shard_map/ppermute | solution.py:17
  52.1 8.6 %collective-permute-start.5 = (f32[2,1,256,128]{3,2,1,0:T(8,128)S(1)}, f32[2,1,256,128]{3,2,1,0:T(8,128)S(1)}, u32[]{:S(2)}, u32[]{:S(2)}) collective-permute-start(f32[2,1,256,128]{3,2,1,0:T(8,128)S(1)} %slice.898), channel_id=1, source_target_pairs={{0,1},{1,2},{2,3},{3,4},{4,5},{5,6},{6,7},{7,8},{8,9},{9,10},{10,1... | collective-permute-start | bytes 786440 | tf_op jit(solution)/shard_map/ppermute | solution.py:17
  63.4 5.1 %collective-permute-start.6 = (f32[2,1,256,128]{3,2,1,0:T(8,128)S(1)}, f32[2,1,256,128]{3,2,1,0:T(8,128)S(1)}, u32[]{:S(2)}, u32[]{:S(2)}) collective-permute-start(f32[2,1,256,128]{3,2,1,0:T(8,128)S(1)} %slice.911), channel_id=1, source_target_pairs={{1,0},{2,1},{3,2},{4,3},{5,4},{6,5},{7,6},{8,7},{9,8},{10,9},{11,1... | collective-permute-start | bytes 786440 | tf_op jit(solution)/shard_map/ppermute | solution.py:17
  69.5 8.6 %collective-permute-start.7 = (f32[2,1,256,128]{3,2,1,0:T(8,128)S(1)}, f32[2,1,256,128]{3,2,1,0:T(8,128)S(1)}, u32[]{:S(2)}, u32[]{:S(2)}) collective-permute-start(f32[2,1,256,128]{3,2,1,0:T(8,128)S(1)} %slice.922), channel_id=1, source_target_pairs={{0,1},{1,2},{2,3},{3,4},{4,5},{5,6},{6,7},{7,8},{8,9},{9,10},{10,1... | collective-permute-start | bytes 786440 | tf_op jit(solution)/shard_map/ppermute | solution.py:17
  80.7 5.1 %collective-permute-start.8 = (f32[2,1,256,128]{3,2,1,0:T(8,128)S(1)}, f32[2,1,256,128]{3,2,1,0:T(8,128)S(1)}, u32[]{:S(2)}, u32[]{:S(2)}) collective-permute-start(f32[2,1,256,128]{3,2,1,0:T(8,128)S(1)} %slice.935), channel_id=1, source_target_pairs={{1,0},{2,1},{3,2},{4,3},{5,4},{6,5},{7,6},{8,7},{9,8},{10,9},{11,1... | collective-permute-start | bytes 786440 | tf_op jit(solution)/shard_map/ppermute | solution.py:17
  87.0 9.1 %collective-permute-start.9 = (f32[2,1,256,128]{3,2,1,0:T(8,128)S(1)}, f32[2,1,256,128]{3,2,1,0:T(8,128)S(1)}, u32[]{:S(2)}, u32[]{:S(2)}) collective-permute-start(f32[2,1,256,128]{3,2,1,0:T(8,128)S(1)} %slice.946), channel_id=1, source_target_pairs={{0,1},{1,2},{2,3},{3,4},{4,5},{5,6},{6,7},{7,8},{8,9},{9,10},{10,1... | collective-permute-start | bytes 786440 | tf_op jit(solution)/shard_map/ppermute | solution.py:17
  98.5 5.1 %collective-permute-start.10 = (f32[2,1,256,128]{3,2,1,0:T(8,128)S(1)}, f32[2,1,256,128]{3,2,1,0:T(8,128)S(1)}, u32[]{:S(2)}, u32[]{:S(2)}) collective-permute-start(f32[2,1,256,128]{3,2,1,0:T(8,128)S(1)} %slice.959), channel_id=1, source_target_pairs={{1,0},{2,1},{3,2},{4,3},{5,4},{6,5},{7,6},{8,7},{9,8},{10,9},{11,1... | collective-permute-start | bytes 786440 | tf_op jit(solution)/shard_map/ppermute | solution.py:17
  104.7 9.6 %copy-start.2 = (f32[3,4,256,128]{3,2,1,0:T(8,128)}, f32[3,4,256,128]{3,2,1,0:T(8,128)S(1)}, u32[]{:S(2)}) copy-start(f32[3,4,256,128]{3,2,1,0:T(8,128)S(1)} %fusion.15) | copy-start | bytes 4718596
  104.8 9.5 %collective-permute-start.11 = (f32[2,1,256,128]{3,2,1,0:T(8,128)S(1)}, f32[2,1,256,128]{3,2,1,0:T(8,128)S(1)}, u32[]{:S(2)}, u32[]{:S(2)}) collective-permute-start(f32[2,1,256,128]{3,2,1,0:T(8,128)S(1)} %slice.970), channel_id=1, source_target_pairs={{0,1},{1,2},{2,3},{3,4},{4,5},{5,6},{6,7},{7,8},{8,9},{9,10},{10,1... | collective-permute-start | bytes 786440 | tf_op jit(solution)/shard_map/ppermute | solution.py:17
  116.4 8.8 %copy-start.3 = (f32[3,4,256,128]{3,2,1,0:T(8,128)}, f32[3,4,256,128]{3,2,1,0:T(8,128)S(1)}, u32[]{:S(2)}) copy-start(f32[3,4,256,128]{3,2,1,0:T(8,128)S(1)} %fusion.17) | copy-start | bytes 4718596
  118.2 40.2 %copy-start.4 = (f32[2,4,8,4,4,256]{5,4,3,2,1,0:T(4,128)}, f32[2,4,8,4,4,256]{5,4,3,2,1,0:T(4,128)S(1)}, u32[]{:S(2)}) copy-start(f32[2,4,8,4,4,256]{5,4,3,2,1,0:T(4,128)S(1)} %multiply_add_fusion) | copy-start | bytes 3145732
where the time goes:
time: 159 us; the launch traced here: 158 us
  starting transfers between devices  49.9 us (31%)
  blocking collectives  33.2 us (21%)
  other arithmetic  22.6 us (14%)
  waiting for transfers between devices  21 us (13%)
  matrix products  13.9 us (9%)
  local copies, waits for them, and re-layouts  12.2 us (8%)
  between operations  5.55 us (3%)
    ppermute x12, starting transfers between devices, shifted(): lax.ppermute(value, axis, [(source, source + steps) for source in range(f...  49.9 us
    psum x1, blocking collectives, on_device(): intersection = lax.psum(partial_value, 'gx')  33.2 us
    ppermute x12, waiting for transfers between devices, shifted(): lax.ppermute(value, axis, [(source, source + steps) for source in range(f...  21 us
    dot_general x1, matrix products, project(): jnp.einsum('rcfmxy,cmxy->rmf', monitors, pairing, precision=lax.Precision...  6.99 us
    add x6, other arithmetic, pole_update(): e_field = e_field + step_e * (curl_field - current)  5.96 us
    mul x1, other arithmetic, pole_update(): current = retain * current + pulling * e_field - spring * polarized  4.4 us
    another operation x6, other arithmetic, curl_h(): return jnp.stack([first, second, third])  4.26 us
    dot_general x6, matrix products, record(): jnp.einsum('cxyz,zm->cmxy', h_field[:2], select, precision=lax.Precision....  3.47 us
  transfers between devices with their start and end apart: 12, of which 11 were waited for; matrix products, arithmetic and copies ran while one was open for 11% of the time, Pallas kernels for 0%

commit v1 on v0

v1 whole, which is shorter than its diff:
```python
import functools
import math

import jax
import jax.numpy as jnp
from jax import lax
from jax.experimental import pallas as pl
from jax.experimental.pallas import tpu as pltpu
from jax.sharding import PartitionSpec as P

STEPS = 6
DT = 0.5
CHUNKS = 4
ROWS = 32
PAD = 8
MESH = pl.DeviceIdType.MESH
F32 = jnp.float32
BF16 = jnp.bfloat16


def ahead(value):
    width = value.shape[-1]
    lane = lax.broadcasted_iota(jnp.int32, value.shape, 1)
    return jnp.where(lane == width - 1, 0.0, pltpu.roll(value, width - 1, 1))


def behind(value):
    lane = lax.broadcasted_iota(jnp.int32, value.shape, 1)
    return jnp.where(lane == 0, 0.0, pltpu.roll(value, 1, 1))


def main_kernel(
    count,
    scale,
    perm_ref,
    freq_ref,
    damp_ref,
    strength_ref,
    depth_ref,
    rot_ref,
    rotv_ref,
    mode_ref,
    el_ref,
    ma_ref,
    mat_ref,
    el_out,
    ma_out,
    mon_ref,
    inter_ref,
    eb,
    hb,
    ge,
    gh,
    jb,
    pb,
    coef,
    matb,
    planes,
    pick,
    part,
    gathered,
    in_sem,
    out_sem,
    se_sem,
    re_sem,
    sh_sem,
    rh_sem,
    sp_sem,
    rp_sem,
):
    me = lax.axis_index("gx")
    layers, width = mat_ref.shape[0], mat_ref.shape[1]
    chunk = width // CHUNKS
    has_upper = me < count - 1
    has_lower = me > 0
    top = layers - 1

    barrier = pltpu.get_barrier_semaphore()
    for k in range(1, count):
        pl.semaphore_signal(
            barrier, inc=1, device_id={"gx": lax.rem(me + k, count)}, device_id_type=MESH
        )

    loads = [
        pltpu.make_async_copy(mat_ref, matb, in_sem.at[0]),
        pltpu.make_async_copy(el_ref, eb.at[:, :, pl.ds(0, width)], in_sem.at[1]),
        pltpu.make_async_copy(ma_ref, hb.at[:, :, pl.ds(PAD, width)], in_sem.at[2]),
    ]
    for load in loads:
        load.start()

    def send_e(c, source):
        rows = pl.ds(c * chunk, chunk)
        return pltpu.make_async_remote_copy(
            src_ref=source.at[pl.ds(1, 2), 0, rows],
            dst_ref=ge.at[:, rows],
            send_sem=se_sem.at[c],
            recv_sem=re_sem.at[c],
            device_id={"gx": me - 1},
            device_id_type=MESH,
        )

    def send_h(c):
        return pltpu.make_async_remote_copy(
            src_ref=hb.at[pl.ds(1, 2), top, pl.ds(PAD + c * chunk, chunk)],
            dst_ref=gh.at[:, pl.ds(c * chunk, chunk)],
            send_sem=sh_sem.at[c],
            recv_sem=rh_sem.at[c],
            device_id={"gx": me + 1},
            device_id_type=MESH,
        )

    nm = depth_ref.shape[0]
    deep = mat_ref.shape[2]
    shape = pick.shape
    row = lax.broadcasted_iota(jnp.int32, shape, 0)
    col = lax.broadcasted_iota(jnp.int32, shape, 1)
    wanted = jnp.zeros(shape, jnp.int32)
    for m in range(nm):
        wanted = jnp.where(row // 8 == m, depth_ref[m], wanted)
    hit = (row % 8 == col // (2 * deep)) & (col % deep == wanted)
    pick[...] = jnp.where(hit, 1.0, 0.0).astype(BF16)

    zero_rows = jnp.zeros((PAD, deep), F32)
    for c in range(3):
        for x in range(layers):
            eb[c, x, pl.ds(width, PAD), :] = zero_rows
            hb[c, x, pl.ds(0, PAD), :] = zero_rows

    @pl.when(jnp.logical_not(has_upper))
    def _():
        ge[...] = jnp.zeros_like(ge)

    @pl.when(jnp.logical_not(has_lower))
    def _():
        gh[...] = jnp.zeros_like(gh)

    kinds = perm_ref.shape[0]
    offset = kinds - freq_ref.shape[0]
    ones = jnp.ones((8, deep), F32)
    tables = []
    for kind in range(kinds):
        if kind < offset:
            g, w2, drive = 0.0 * ones, 0.0 * ones, 0.0 * ones
        else:
            p = kind - offset
            g = damp_ref[p] * ones
            w2 = (freq_ref[p] * ones) * freq_ref[p]
            drive = strength_ref[p] * w2
        divisor = 1.0 + 0.5 * DT * g
        tables.append(
            (
                (1.0 - 0.5 * DT * g) / divisor,
                DT * drive / divisor,
                DT * w2 / divisor,
                DT / (perm_ref[kind] * ones),
            )
        )

    loads[0].wait()
    for x in range(layers):

        def fill(b, carry, x=x):
            rows = pl.ds(pl.multiple_of(b * 8, 8), 8)
            q = matb[x, rows, :]
            for i in range(4):
                value = tables[0][i]
                for kind in range(1, kinds):
                    value = jnp.where(q == kind, tables[kind][i], value)
                coef[i, x, rows, :] = value
            zero = jnp.zeros_like(ones)
            for c in range(3):
                jb[c, x, rows, :] = zero
                pb[c, x, rows, :] = zero
            return carry

        lax.fori_loop(0, width // 8, fill, 0, unroll=2)

    pl.semaphore_wait(barrier, count - 1)

    @pl.when(has_lower)
    def _():
        for c in range(CHUNKS):
            send_e(c, el_ref).start()

    loads[1].wait()
    loads[2].wait()

    def update_h(x, y):
        here, next_y = pl.ds(y, ROWS), pl.ds(y + 1, ROWS)
        spot = pl.ds(y + PAD, ROWS)
        ex, ey, ez = eb[0, x, here, :], eb[1, x, here, :], eb[2, x, here, :]
        ex_y, ez_y = eb[0, x, next_y, :], eb[2, x, next_y, :]
        if x < top:
            ey_x, ez_x = eb[1, x + 1, here, :], eb[2, x + 1, here, :]
        else:
            ey_x, ez_x = ge[0, here, :], ge[1, here, :]
        hb[0, x, spot, :] -= DT * ((ez_y - ez) - (ahead(ey) - ey))
        hb[1, x, spot, :] -= DT * ((ahead(ex) - ex) - (ez_x - ez))
        hb[2, x, spot, :] -= DT * ((ey_x - ey) - (ex_y - ex))

    def update_e(x, y):
        here = pl.ds(y, ROWS)
        spot, last_y = pl.ds(y + PAD, ROWS), pl.ds(y + PAD - 1, ROWS)
        hx, hy, hz = hb[0, x, spot, :], hb[1, x, spot, :], hb[2, x, spot, :]
        hx_y, hz_y = hb[0, x, last_y, :], hb[2, x, last_y, :]
        if x > 0:
            hy_x, hz_x = hb[1, x - 1, spot, :], hb[2, x - 1, spot, :]
        else:
            hy_x, hz_x = gh[0, here, :], gh[1, here, :]
        curl = (
            (hz - hz_y) - (hy - behind(hy)),
            (hx - behind(hx)) - (hz - hz_x),
            (hy - hy_x) - (hx - hx_y),
        )
        retain, pulling = coef[0, x, here, :], coef[1, x, here, :]
        spring, step_e = coef[2, x, here, :], coef[3, x, here, :]
        for c in range(3):
            field, polar = eb[c, x, here, :], pb[c, x, here, :]
            current = retain * jb[c, x, here, :] + pulling * field - spring * polar
            jb[c, x, here, :] = current
            pb[c, x, here, :] = polar + DT * current
            eb[c, x, here, :] = field + step_e * (curl[c] - current)

    def over(update, xs, start, size):
        def body(b, carry):
            y = pl.multiple_of(start + b * ROWS, ROWS)
            for x in xs:
                update(x, y)
            return carry

        lax.fori_loop(0, size // ROWS, body, 0)

    def record(n, buf, base, first):
        for c in range(2):
            total = jnp.zeros((pick.shape[0], width), F32)
            for x in range(layers):
                value = buf[c, x, pl.ds(base, width), :]
                high = value.astype(BF16)
                low = (value - high.astype(F32)).astype(BF16)
                total = total + lax.dot_general(
                    pick[:, pl.ds(x * 2 * deep, 2 * deep)],
                    jnp.concatenate([high, low], axis=1),
                    (((1,), (1,)), ((), ())),
                    preferred_element_type=F32,
                )
            planes[n, first + c] = total

    def step(n, carry):
        over(update_h, range(top), 0, width)
        for c in range(CHUNKS):

            @pl.when(has_upper)
            def _(c=c):
                send_e(c, eb).wait_recv()

                @pl.when(n > 0)
                def _():
                    send_h(c).wait_send()

            over(update_h, [top], c * chunk, chunk)

            @pl.when(has_upper)
            def _(c=c):
                send_h(c).start()

        record(n, hb, PAD, 2)
        over(update_e, range(1, layers), 0, width)
        for c in range(CHUNKS):

            @pl.when(has_lower)
            def _(c=c):
                send_h(c).wait_recv()
                send_e(c, eb).wait_send()

            over(update_e, [0], c * chunk, chunk)

            @pl.when(has_lower & (n < STEPS - 1))
            def _(c=c):
                send_e(c, eb).start()

        record(n, eb, 0, 0)
        return carry

    lax.fori_loop(0, STEPS, step, 0)

    @pl.when(has_upper)
    def _():
        for c in range(CHUNKS):
            send_h(c).wait_send()

    stores = [
        pltpu.make_async_copy(eb.at[:, :, pl.ds(0, width)], el_out, out_sem.at[0]),
        pltpu.make_async_copy(hb.at[:, :, pl.ds(PAD, width)], ma_out, out_sem.at[1]),
    ]
    for store in stores:
        store.start()

    lane = lax.broadcasted_iota(jnp.int32, (nm, deep), 1)
    total = jnp.zeros((nm, deep), F32)
    for c in range(4):
        weights = [mode_ref[3 - c, m] for m in range(nm)]
        for n in range(STEPS):
            sums = []
            for m in range(nm):
                product = planes[n, c, pl.ds(8 * m, layers), :] * weights[m]
                sums.append(jnp.sum(product, axis=0, keepdims=True))
            value = jnp.sum(jnp.concatenate(sums, axis=0), axis=1, keepdims=True)
            value = value if c in (0, 3) else -value
            total = jnp.where(lane == n * 4 + c, value, total)
    part[pl.ds(0, nm), :] = total
    part[pl.ds(nm, 8 - nm), :] = jnp.zeros((8 - nm, deep), F32)

    def share(k, slot):
        return pltpu.make_async_remote_copy(
            src_ref=part,
            dst_ref=gathered.at[slot],
            send_sem=sp_sem.at[k],
            recv_sem=rp_sem.at[k],
            device_id={"gx": lax.rem(me + k, count)},
            device_id_type=MESH,
        )

    for k in range(1, count):
        share(k, me).start()
    gathered[me] = part[...]

    nf = rot_ref.shape[1] // (2 * STEPS)
    for c in range(4):
        half = c // 2
        for m in range(nm):
            plane = [planes[n, c, pl.ds(8 * m, layers), :] for n in range(STEPS)]
            for r in range(2):
                for f in range(nf):
                    value = rot_ref[r, (half * STEPS) * nf + f] * plane[0]
                    for n in range(1, STEPS):
                        value = value + rot_ref[r, (half * STEPS + n) * nf + f] * plane[n]
                    mon_ref[r, c, f, m] = value

    for k in range(1, count):
        share(k, lax.rem(me - k + count, count)).wait()
    full = gathered[0]
    for k in range(1, count):
        full = full + gathered[k]
    for r in range(2):
        out = lax.dot_general(
            full,
            rotv_ref[r],
            (((1,), (1,)), ((), ())),
            preferred_element_type=F32,
            precision=lax.Precision.HIGHEST,
        )
        inter_ref[r] = scale * out[:nm, :]
    for store in stores:
        store.wait()


def on_device(
    electric,
    magnetic,
    material,
    permittivity,
    pole_frequency,
    pole_damping,
    pole_strength,
    frequencies,
    plane_depth,
    mode_fields,
):
    count = lax.axis_size("gx")
    layers, width, deep = material.shape
    nm, nf = plane_depth.shape[0], frequencies.shape[0]
    scale = 1.0 / math.sqrt(4.0 * layers * count * width)
    step = jnp.arange(STEPS, dtype=F32)
    times = jnp.stack([(step + 1.0) * DT, (step + 0.5) * DT])
    phase = times[:, :, None] * frequencies[None, None, :]
    rot = jnp.stack([jnp.cos(phase), -jnp.sin(phase)])
    table = rot.reshape(2, 2 * STEPS * nf)
    lanes = jnp.repeat(rot, 2, axis=1).transpose(0, 3, 2, 1).reshape(2, nf, STEPS * 4)
    lanes = jnp.pad(lanes, ((0, 0), (0, 0), (0, deep - STEPS * 4)))

    smem = pl.BlockSpec(memory_space=pltpu.SMEM)
    vmem = pl.BlockSpec(memory_space=pltpu.VMEM)
    hbm = pl.BlockSpec(memory_space=pl.ANY)
    field = (3, layers, width, deep)
    dma = pltpu.SemaphoreType.DMA
    return pl.pallas_call(
        functools.partial(main_kernel, count, scale),
        out_shape=(
            jax.ShapeDtypeStruct(field, F32),
            jax.ShapeDtypeStruct(field, F32),
            jax.ShapeDtypeStruct((2, 4, nf, nm, layers, width), F32),
            jax.ShapeDtypeStruct((2, nm, nf), F32),
        ),
        in_specs=[smem] * 6 + [vmem] * 2 + [hbm] * 3,
        out_specs=(hbm, hbm, vmem, vmem),
        scratch_shapes=[
            pltpu.VMEM((3, layers, width + PAD, deep), F32),
            pltpu.VMEM((3, layers, width + PAD, deep), F32),
            pltpu.VMEM((2, width, deep), F32),
            pltpu.VMEM((2, width, deep), F32),
            pltpu.VMEM(field, F32),
            pltpu.VMEM(field, F32),
            pltpu.VMEM((4, layers, width, deep), F32),
            pltpu.VMEM((layers, width, deep), jnp.int32),
            pltpu.VMEM((STEPS, 4, 8 * nm, width), F32),
            pltpu.VMEM((8 * nm, layers * 2 * deep), BF16),
            pltpu.VMEM((8, deep), F32),
            pltpu.VMEM((count, 8, deep), F32),
            dma((3,)),
            dma((2,)),
            dma((CHUNKS,)),
            dma((CHUNKS,)),
            dma((CHUNKS,)),
            dma((CHUNKS,)),
            dma((count,)),
            dma((count,)),
        ],
        compiler_params=pltpu.CompilerParams(collective_id=0, has_side_effects=True),
    )(
        permittivity,
        pole_frequency,
        pole_damping,
        pole_strength,
        plane_depth,
        table,
        lanes,
        mode_fields,
        electric,
        magnetic,
        material,
    )


def solution(mesh):
    in_specs = (
        P(None, "gx", None, None),
        P(None, "gx", None, None),
        P(("member", "gx"), None, None),
        P(),
        P(),
        P(),
        P(),
        P(),
        P(),
        P(None, None, "gx", None),
    )
    out_specs = (
        P(None, ("member", "gx"), None, None),
        P(None, ("member", "gx"), None, None),
        P(None, None, None, None, ("member", "gx"), None),
        P("member", None, None),
    )
    return jax.shard_map(
        on_device, mesh=mesh, in_specs=in_specs, out_specs=out_specs, check_vma=False
    )
```

time: 159 us -> 65.6 us (0.41)
  Pallas kernels: 0 us -> 55.4 us
  starting transfers between devices: 49.9 us -> 0 us
  blocking collectives: 33.2 us -> 0 us
  waiting for transfers between devices: 21 us -> 0 us
  other arithmetic: 22.6 us -> 2.2 us
  matrix products: 13.9 us -> 0 us
  local copies, waits for them, and re-layouts: 12.2 us -> 7.07 us
  between operations: 5.55 us -> 0.69 us
    pallas_call x0 -> x1, Pallas kernels: none -> 55.4 us  [on_device(): pl.pallas_call(functools.partial(main_kernel, count, scale), out_shape=(j...]
    ppermute x12 -> x0, starting transfers between devices: 49.9 us -> none  [shifted(): lax.ppermute(value, axis, [(source, source + steps) for source in range(f...]
    psum x1 -> x0, blocking collectives: 33.2 us -> none  [on_device(): intersection = lax.psum(partial_value, 'gx')]
    ppermute x12 -> x0, waiting for transfers between devices: 21 us -> none  [shifted(): lax.ppermute(value, axis, [(source, source + steps) for source in range(f...]
    dot_general x13 -> x0, matrix products: 13.9 us -> none  [the longest x1 6.99 us: project(): jnp.einsum('rcfmxy,cmxy->rmf', monitors, pairing, precision=lax.Precision...]
    slice x52 -> x0, local copies, waits for them, and re-layouts: 7.17 us -> none  [the longest x30 3.17 us: diff_ahead(): lax.slice_in_dim(field, 1, field.shape[direction], axis=direction)]
    add x7 -> x0, other arithmetic: 7.08 us -> none  [the longest x6 5.96 us: pole_update(): e_field = e_field + step_e * (curl_field - current)]
    another operation x23 -> x3, other arithmetic: 6.4 us -> 0.59 us  [the longest x2 0.59 us: on_device(): rot = jnp.stack([jnp.cos(phase), -jnp.sin(phase)])]
  transfers between devices with their start and end apart: 12 -> 0, of which waited for: 11 -> 0; matrix products, arithmetic and copies ran while one was open for 11% -> 0% of each run, Pallas kernels for 0% -> 0%
where the time goes in v1:
time: 65.6 us; the launch traced here: 65.4 us
  Pallas kernels  55.4 us (84%)
  local copies, waits for them, and re-layouts  7.07 us (11%)
  other arithmetic  2.2 us (3%)
  between operations  0.69 us (1%)
    pallas_call x1, Pallas kernels, on_device(): pl.pallas_call(functools.partial(main_kernel, count, scale), out_shape=(j...  55.4 us
    unnamed x10, local copies, waits for them, and re-layouts  6.13 us
    cos x2, other arithmetic, on_device(): rot = jnp.stack([jnp.cos(phase), -jnp.sin(phase)])  1.59 us

profile of v1, /device:TPU:0, one launch (start us, length us, event | category | flops | bytes accessed | tf_op | source)
XLA Modules:
  0.0 65.4 jit_solution(12924743347747746169)
XLA Ops:
  0.7 0.1 copy.15
  0.8 0.8 %multiply_cosine_fusion.1 = (f32[1,2,6,8]{3,1,2,0:T(2,128)S(1)}, f32[1,2,6,8]{3,1,2,0:T(2,128)S(1)}) fusion(f32[8]{0:T(128)} %param.17, f32[2,6]{0,1:T(8,128)S(1)} %copy.15), kind=kLoop, calls=%fused_computation.5 | loop fusion | flops 192 | bytes 848 | tf_op jit(solution)/shard_map/cos | solution.py:377
  1.6 0.1 copy.16
  1.7 0.6 pad.4.rotv_ref
  2.3 0.8 %multiply_cosine_fusion = (f32[2,6,8]{2,1,0:T(8,128)S(1)}, f32[2,6,8]{2,1,0:T(8,128)S(1)}) fusion(f32[8]{0:T(128)} %param.17, f32[2,6]{1,0:T(2,128)S(1)} %pad_maximum_fusion.1), kind=kLoop, calls=%fused_computation.2 | loop fusion | flops 192 | bytes 848 | tf_op jit(solution)/shard_map/cos | solution.py:377
  3.1 0.1 cos.23
  3.1 0.1 neg.23
  3.2 0.6 pad_maximum_fusion.2.rot_ref
  3.8 55.4 %shard_map.129 = (f32[3,4,256,128]{3,2,1,0:T(8,128)}, f32[3,4,256,128]{3,2,1,0:T(8,128)}, f32[2,4,8,4,4,256]{5,4,3,2,1,0:T(4,128)}, f32[2,4,8]{2,1,0:T(4,128)}) custom-call(f32[4]{0:T(128)} %perm_ref.1, f32[2]{0:T(128)} %freq_ref.1, f32[2]{0:T(128)} %damp_ref.1, f32[2]{0:T(128)} %strength_ref.1, s32[4]{0:T(128)} %depth_ref.1, ...), custom_call_target="tpu_custom_call" | custom-call | tf_op jit(solution)/shard_map/pallas_call | solution.py:387
  59.2 0.0 copy-start
  59.2 2.8 %copy.21 = f32[3,4,256,128]{3,2,1,0:T(8,128)} copy(f32[3,4,256,128]{3,2,1,0:T(8,128)} %get-tuple-element.14) | data formatting | bytes 3145728
  62.0 0.0 copy-done
  62.0 0.0 copy-start.1
  62.0 1.1 %copy.22 = f32[3,4,256,128]{3,2,1,0:T(8,128)} copy(f32[3,4,256,128]{3,2,1,0:T(8,128)S(1)} %copy-done) | data formatting | bytes 3145728
  63.2 0.6 copy-done.1
  63.8 0.0 copy-start.2
  63.8 1.0 %copy.23 = f32[2,4,8,4,4,256]{5,4,3,2,1,0:T(4,128)} copy(f32[2,4,8,4,4,256]{5,4,3,2,1,0:T(4,128)S(1)} %copy-done.1) | data formatting | bytes 2097152
  64.8 0.0 copy-done.2
  64.8 0.6 copy.24
  (4 shorter events, 0.0 us)
Async XLA Ops:
  59.2 2.8 %copy-start = (f32[3,4,256,128]{3,2,1,0:T(8,128)S(1)}, f32[3,4,256,128]{3,2,1,0:T(8,128)}, u32[]{:S(2)}) copy-start(f32[3,4,256,128]{3,2,1,0:T(8,128)} %get-tuple-element.15) | copy-start | bytes 4718596
  62.0 1.8 %copy-start.1 = (f32[2,4,8,4,4,256]{5,4,3,2,1,0:T(4,128)S(1)}, f32[2,4,8,4,4,256]{5,4,3,2,1,0:T(4,128)}, u32[]{:S(2)}) copy-start(f32[2,4,8,4,4,256]{5,4,3,2,1,0:T(4,128)} %get-tuple-element.16) | copy-start | bytes 3145732
  63.8 1.0 %copy-start.2 = (f32[2,4,8]{2,1,0:T(4,128)S(1)}, f32[2,4,8]{2,1,0:T(4,128)}, u32[]{:S(2)}) copy-start(f32[2,4,8]{2,1,0:T(4,128)} %get-tuple-element.17) | copy-start | bytes 772

commit v2 on v1

v2 whole, which is shorter than its diff:
```python
import functools
import math

import jax
import jax.numpy as jnp
from jax import lax
from jax.experimental import pallas as pl
from jax.experimental.pallas import tpu as pltpu
from jax.sharding import PartitionSpec as P

STEPS = 6
DT = 0.5
CHUNKS = 8
ROWS = 32
PAD = 8
MESH = pl.DeviceIdType.MESH
VMEM_BYTES = 67043328
F32 = jnp.float32
BF16 = jnp.bfloat16


def ahead(value):
    width = value.shape[-1]
    lane = lax.broadcasted_iota(jnp.int32, value.shape, 1)
    return jnp.where(lane == width - 1, 0.0, pltpu.roll(value, width - 1, 1))


def behind(value):
    lane = lax.broadcasted_iota(jnp.int32, value.shape, 1)
    return jnp.where(lane == 0, 0.0, pltpu.roll(value, 1, 1))


def main_kernel(
    count,
    scale,
    perm_ref,
    freq_ref,
    damp_ref,
    strength_ref,
    omega_ref,
    depth_ref,
    mode_ref,
    el_ref,
    ma_ref,
    mat_ref,
    eb,
    hb,
    mon_ref,
    inter_ref,
    ge,
    gh,
    jb,
    pb,
    coef,
    matb,
    planes,
    pick,
    part,
    gathered,
    rot,
    rot_s,
    in_sem,
    rot_sem,
    se_sem,
    re_sem,
    sh_sem,
    rh_sem,
    sp_sem,
    rp_sem,
):
    me = lax.axis_index("gx")
    layers, width, deep = mat_ref.shape
    nm, nf = depth_ref.shape[0], omega_ref.shape[0]
    chunk = width // CHUNKS
    has_upper = me < count - 1
    has_lower = me > 0
    top = layers - 1

    barrier = pltpu.get_barrier_semaphore()
    for k in range(1, count):
        pl.semaphore_signal(
            barrier, inc=1, device_id={"gx": lax.rem(me + k, count)}, device_id_type=MESH
        )

    loads = [
        pltpu.make_async_copy(el_ref, eb.at[:, :, pl.ds(0, width)], in_sem.at[0]),
        pltpu.make_async_copy(ma_ref, hb.at[:, :, pl.ds(PAD, width)], in_sem.at[1]),
        pltpu.make_async_copy(mat_ref, matb, in_sem.at[2]),
    ]
    for load in loads:
        load.start()

    def send_e(c, source):
        rows = pl.ds(c * chunk, chunk)
        return pltpu.make_async_remote_copy(
            src_ref=source.at[pl.ds(1, 2), 0, rows],
            dst_ref=ge.at[:, rows],
            send_sem=se_sem.at[c],
            recv_sem=re_sem.at[c],
            device_id={"gx": me - 1},
            device_id_type=MESH,
        )

    def send_h(c):
        return pltpu.make_async_remote_copy(
            src_ref=hb.at[pl.ds(1, 2), top, pl.ds(PAD + c * chunk, chunk)],
            dst_ref=gh.at[:, pl.ds(c * chunk, chunk)],
            send_sem=sh_sem.at[c],
            recv_sem=rh_sem.at[c],
            device_id={"gx": me + 1},
            device_id_type=MESH,
        )

    shape = pick.shape
    row = lax.broadcasted_iota(jnp.int32, shape, 0)
    col = lax.broadcasted_iota(jnp.int32, shape, 1)
    wanted = jnp.zeros(shape, jnp.int32)
    for m in range(nm):
        wanted = jnp.where(row // 8 == m, depth_ref[m], wanted)
    hit = (row % 8 == col // (2 * deep)) & (col % deep == wanted)
    pick[...] = jnp.where(hit, 1.0, 0.0).astype(BF16)

    lane = lax.broadcasted_iota(jnp.int32, (nf, deep), 1)
    line = lax.broadcasted_iota(jnp.int32, (nf, deep), 0)
    omega = jnp.zeros((nf, deep), F32)
    for f in range(nf):
        omega = jnp.where(line == f, omega_ref[f], omega)
    late = jnp.where(lane % 4 < 2, 1.0, 0.5)
    phase = ((lane // 4).astype(F32) + late) * DT * omega
    rot[0] = jnp.where(lane < 4 * STEPS, jnp.cos(phase), 0.0)
    rot[1] = jnp.where(lane < 4 * STEPS, -jnp.sin(phase), 0.0)

    zero_rows = jnp.zeros((PAD, deep), F32)
    for c in range(3):
        for x in range(layers):
            eb[c, x, pl.ds(width, PAD), :] = zero_rows
            hb[c, x, pl.ds(0, PAD), :] = zero_rows
    part[...] = jnp.zeros_like(part)

    pl.semaphore_wait(barrier, count - 1)

    @pl.when(has_lower)
    def _():
        for c in range(CHUNKS):
            send_e(c, el_ref).start()

    kinds = perm_ref.shape[0]
    offset = kinds - freq_ref.shape[0]
    ones = jnp.ones((8, deep), F32)
    tables = []
    for kind in range(kinds):
        if kind < offset:
            g, w2, drive = 0.0 * ones, 0.0 * ones, 0.0 * ones
        else:
            p = kind - offset
            g = damp_ref[p] * ones
            w2 = (freq_ref[p] * ones) * freq_ref[p]
            drive = strength_ref[p] * w2
        divisor = 1.0 + 0.5 * DT * g
        tables.append(
            (
                (1.0 - 0.5 * DT * g) / divisor,
                DT * drive / divisor,
                DT * w2 / divisor,
                DT / (perm_ref[kind] * ones),
            )
        )

    loads[2].wait()
    for x in range(layers):

        def fill(b, carry, x=x):
            rows = pl.ds(pl.multiple_of(b * 8, 8), 8)
            q = matb[x, rows, :]
            for i in range(4):
                value = tables[0][i]
                for kind in range(1, kinds):
                    value = jnp.where(q == kind, tables[kind][i], value)
                coef[i, x, rows, :] = value
            zero = jnp.zeros_like(ones)
            for c in range(3):
                jb[c, x, rows, :] = zero
                pb[c, x, rows, :] = zero
            return carry

        lax.fori_loop(0, width // 8, fill, 0, unroll=2)

    loads[0].wait()
    loads[1].wait()

    def update_h(x, y, size):
        here, next_y = pl.ds(y, size), pl.ds(y + 1, size)
        spot = pl.ds(y + PAD, size)
        ex, ey, ez = eb[0, x, here, :], eb[1, x, here, :], eb[2, x, here, :]
        ex_y, ez_y = eb[0, x, next_y, :], eb[2, x, next_y, :]
        hb[0, x, spot, :] -= DT * ((ez_y - ez) - (ahead(ey) - ey))
        if x < top:
            ey_x, ez_x = eb[1, x + 1, here, :], eb[2, x + 1, here, :]
            hb[1, x, spot, :] -= DT * ((ahead(ex) - ex) - (ez_x - ez))
            hb[2, x, spot, :] -= DT * ((ey_x - ey) - (ex_y - ex))
        else:
            hb[1, x, spot, :] -= DT * ((ahead(ex) - ex) + ez)
            hb[2, x, spot, :] += DT * (ey + (ex_y - ex))

    def finish_h(y, size):
        here, spot = pl.ds(y, size), pl.ds(y + PAD, size)
        hb[1, top, spot, :] += DT * ge[1, here, :]
        hb[2, top, spot, :] -= DT * ge[0, here, :]

    def update_e(x, y, size):
        here = pl.ds(y, size)
        spot, last_y = pl.ds(y + PAD, size), pl.ds(y + PAD - 1, size)
        hx, hy, hz = hb[0, x, spot, :], hb[1, x, spot, :], hb[2, x, spot, :]
        hx_y, hz_y = hb[0, x, last_y, :], hb[2, x, last_y, :]
        if x > 0:
            dz = hz - hb[2, x - 1, spot, :]
            dy = hy - hb[1, x - 1, spot, :]
        else:
            dz, dy = hz, hy
        curl = (
            (hz - hz_y) - (hy - behind(hy)),
            (hx - behind(hx)) - dz,
            dy - (hx - hx_y),
        )
        retain, pulling = coef[0, x, here, :], coef[1, x, here, :]
        spring, step_e = coef[2, x, here, :], coef[3, x, here, :]
        for c in range(3):
            field, polar = eb[c, x, here, :], pb[c, x, here, :]
            current = retain * jb[c, x, here, :] + pulling * field - spring * polar
            jb[c, x, here, :] = current
            pb[c, x, here, :] = polar + DT * current
            eb[c, x, here, :] = field + step_e * (curl[c] - current)

    def finish_e(y, size):
        here = pl.ds(y, size)
        step_e = coef[3, 0, here, :]
        eb[1, 0, here, :] += step_e * gh[1, here, :]
        eb[2, 0, here, :] -= step_e * gh[0, here, :]

    def edge(update, x):
        def body(b, carry):
            update(x, pl.multiple_of(b * ROWS, ROWS), ROWS)
            return carry

        lax.fori_loop(0, width // ROWS, body, 0)

    def inner(update, xs, c):
        for x in xs:
            for y in range(c * chunk, (c + 1) * chunk, min(ROWS, chunk)):
                update(x, y, min(ROWS, chunk))

    def record(n, buf, base, source, c):
        total = jnp.zeros((pick.shape[0], width), F32)
        for x in range(layers):
            value = buf[source, x, pl.ds(base, width), :]
            high = value.astype(BF16)
            low = (value - high.astype(F32)).astype(BF16)
            total = total + lax.dot_general(
                pick[:, pl.ds(x * 2 * deep, 2 * deep)],
                jnp.concatenate([high, low], axis=1),
                (((1,), (1,)), ((), ())),
                preferred_element_type=F32,
            )
        planes[n, c] = total
        sums = []
        for m in range(nm):
            product = total[8 * m : 8 * m + layers, :] * mode_ref[3 - c, m]
            sums.append(jnp.sum(product, axis=0, keepdims=True))
        value = jnp.sum(jnp.concatenate(sums, axis=0), axis=1, keepdims=True)
        value = value if c in (0, 3) else -value
        here = lax.broadcasted_iota(jnp.int32, (nm, deep), 1) == n * 4 + c
        part[pl.ds(0, nm), :] = jnp.where(here, value, part[pl.ds(0, nm), :])

    spots = (CHUNKS // 3, (2 * CHUNKS) // 3)

    def step(n, carry):
        @pl.when(has_upper & (n > 0))
        def _():
            for c in range(CHUNKS):
                send_h(c).wait_send()

        edge(update_h, top)
        for c in range(CHUNKS):

            @pl.when(has_upper)
            def _(c=c):
                send_e(c, eb).wait_recv()
                finish_h(c * chunk, chunk)
                send_h(c).start()

            inner(update_h, range(top), c)
            if c in spots:

                @pl.when(n > 0)
                def _(c=c):
                    record(n - 1, eb, 0, spots.index(c), spots.index(c))

        @pl.when(has_lower)
        def _():
            for c in range(CHUNKS):
                send_e(c, eb).wait_send()

        edge(update_e, 0)
        for c in range(CHUNKS):

            @pl.when(has_lower)
            def _(c=c):
                send_h(c).wait_recv()
                finish_e(c * chunk, chunk)

                @pl.when(n < STEPS - 1)
                def _():
                    send_e(c, eb).start()

            inner(update_e, range(1, layers), c)
            if c in spots:
                record(n, hb, PAD, spots.index(c), 2 + spots.index(c))
        return carry

    lax.fori_loop(0, STEPS, step, 0)

    for c in range(2):
        record(STEPS - 1, eb, 0, c, c)

    def share(k, slot):
        return pltpu.make_async_remote_copy(
            src_ref=part,
            dst_ref=gathered.at[slot],
            send_sem=sp_sem.at[k],
            recv_sem=rp_sem.at[k],
            device_id={"gx": lax.rem(me + k, count)},
            device_id_type=MESH,
        )

    for k in range(1, count):
        share(k, me).start()
    gathered[me] = part[...]

    to_scalars = pltpu.make_async_copy(rot, rot_s, rot_sem)
    to_scalars.start()

    @pl.when(has_upper)
    def _():
        for c in range(CHUNKS):
            send_h(c).wait_send()

    to_scalars.wait()
    for c in range(4):

        def fold(m, carry, c=c):
            rows = pl.ds(pl.multiple_of(8 * m, 8), layers)
            plane = [planes[n, c, rows, :] for n in range(STEPS)]
            for r in range(2):
                for f in range(nf):
                    value = rot_s[r, f, c] * plane[0]
                    for n in range(1, STEPS):
                        value = value + rot_s[r, f, n * 4 + c] * plane[n]
                    mon_ref[r, c, f, m] = value
            return carry

        lax.fori_loop(0, nm, fold, 0)

    for k in range(1, count):
        share(k, lax.rem(me - k + count, count)).wait()
    full = gathered[0]
    for k in range(1, count):
        full = full + gathered[k]
    for r in range(2):
        out = lax.dot_general(
            full,
            rot[r],
            (((1,), (1,)), ((), ())),
            preferred_element_type=F32,
            precision=lax.Precision.HIGHEST,
        )
        inter_ref[r] = scale * out[:nm, :]


def place_kernel(eb, hb, mon, inter, el_out, ma_out, mon_out, inter_out, sems):
    width = el_out.shape[2]
    copies = [
        pltpu.make_async_copy(eb.at[:, :, pl.ds(0, width)], el_out, sems.at[0]),
        pltpu.make_async_copy(hb.at[:, :, pl.ds(PAD, width)], ma_out, sems.at[1]),
        pltpu.make_async_copy(mon, mon_out, sems.at[2]),
        pltpu.make_async_copy(inter, inter_out, sems.at[3]),
    ]
    for copy in copies:
        copy.start()
    for copy in copies:
        copy.wait()


def on_device(
    electric,
    magnetic,
    material,
    permittivity,
    pole_frequency,
    pole_damping,
    pole_strength,
    frequencies,
    plane_depth,
    mode_fields,
):
    count = lax.axis_size("gx")
    layers, width, deep = material.shape
    nm, nf = plane_depth.shape[0], frequencies.shape[0]
    scale = 1.0 / math.sqrt(4.0 * layers * count * width)

    smem = pl.BlockSpec(memory_space=pltpu.SMEM)
    vmem = pl.BlockSpec(memory_space=pltpu.VMEM)
    hbm = pl.BlockSpec(memory_space=pl.ANY)
    field = (3, layers, width, deep)
    padded = (3, layers, width + PAD, deep)
    final = (field, field, (2, 4, nf, nm, layers, width), (2, nm, nf))
    kept = 4 * (2 * math.prod(padded) + math.prod(final[2])) + 2**16
    dma = pltpu.SemaphoreType.DMA
    held = pl.pallas_call(
        functools.partial(main_kernel, count, scale),
        out_shape=tuple(pltpu.VMEM(shape, F32) for shape in (padded, padded) + final[2:]),
        in_specs=[smem] * 6 + [vmem] + [hbm] * 3,
        out_specs=(vmem,) * 4,
        scratch_shapes=[
            pltpu.VMEM((2, width, deep), F32),
            pltpu.VMEM((2, width, deep), F32),
            pltpu.VMEM(field, F32),
            pltpu.VMEM(field, F32),
            pltpu.VMEM((4, layers, width, deep), F32),
            pltpu.VMEM((layers, width, deep), jnp.int32),
            pltpu.VMEM((STEPS, 4, 8 * nm, width), F32),
            pltpu.VMEM((8 * nm, layers * 2 * deep), BF16),
            pltpu.VMEM((8, deep), F32),
            pltpu.VMEM((count, 8, deep), F32),
            pltpu.VMEM((2, nf, deep), F32),
            pltpu.SMEM((2, nf, deep), F32),
            dma((3,)),
            dma,
            dma((CHUNKS,)),
            dma((CHUNKS,)),
            dma((CHUNKS,)),
            dma((CHUNKS,)),
            dma((count,)),
            dma((count,)),
        ],
        compiler_params=pltpu.CompilerParams(
            collective_id=0, has_side_effects=True, vmem_limit_bytes=VMEM_BYTES - kept
        ),
    )(
        permittivity,
        pole_frequency,
        pole_damping,
        pole_strength,
        frequencies,
        plane_depth,
        mode_fields,
        *(pltpu.with_memory_space_constraint(a, pltpu.HBM) for a in (electric, magnetic, material)),
    )
    return pl.pallas_call(
        place_kernel,
        out_shape=tuple(jax.ShapeDtypeStruct(shape, F32) for shape in final),
        in_specs=[vmem] * 4,
        out_specs=(hbm,) * 4,
        scratch_shapes=[dma((4,))],
        compiler_params=pltpu.CompilerParams(vmem_limit_bytes=16 * 2**20),
    )(*held)


def solution(mesh):
    in_specs = (
        P(None, "gx", None, None),
        P(None, "gx", None, None),
        P(("member", "gx"), None, None),
        P(),
        P(),
        P(),
        P(),
        P(),
        P(),
        P(None, None, "gx", None),
    )
    out_specs = (
        P(None, ("member", "gx"), None, None),
        P(None, ("member", "gx"), None, None),
        P(None, None, None, None, ("member", "gx"), None),
        P("member", None, None),
    )
    return jax.shard_map(
        on_device, mesh=mesh, in_specs=in_specs, out_specs=out_specs, check_vma=False
    )
```

time: 65.6 us -> 51.9 us (0.79)
  local copies, waits for them, and re-layouts: 7.07 us -> 0 us
  Pallas kernels: 55.4 us -> 51.1 us
  other arithmetic: 2.2 us -> 0 us
    unnamed x10 -> x0, local copies, waits for them, and re-layouts: 6.13 us -> none
    pallas_call x1 -> x2, Pallas kernels: 55.4 us -> 51.1 us  [the longest x1 49.1 us: on_device(): pl.pallas_call(functools.partial(main_kernel, count, scale), out_shape=tu...]
    cos x2 -> x0, other arithmetic: 1.59 us -> none  [on_device(): rot = jnp.stack([jnp.cos(phase), -jnp.sin(phase)])]
where the time goes in v2:
time: 51.9 us; the launch traced here: 51.8 us
  Pallas kernels  51.1 us (98%)
  between operations  0.64 us (1%)
    pallas_call x1, Pallas kernels, on_device(): pl.pallas_call(functools.partial(main_kernel, count, scale), out_shape=tu...  49.1 us
    pallas_call x1, Pallas kernels, on_device(): pl.pallas_call(place_kernel, out_shape=tuple((jax.ShapeDtypeStruct(shape,...  2.05 us

profile of v2, /device:TPU:0, one launch (start us, length us, event | category | flops | bytes accessed | tf_op | source)
XLA Modules:
  0.0 51.8 jit_solution(13050018036487776110)
XLA Ops:
  0.6 49.1 %shard_map.129 = (f32[3,4,264,128]{3,2,1,0:T(8,128)S(1)}, f32[3,4,264,128]{3,2,1,0:T(8,128)S(1)}, f32[2,4,8,4,4,256]{5,4,3,2,1,0:T(4,128)S(1)}, f32[2,4,8]{2,1,0:T(4,128)S(1)}) custom-call(f32[4]{0:T(128)} %perm_ref.1, f32[2]{0:T(128)} %freq_ref.1, f32[2]{0:T(128)} %damp_ref.1, f32[2]{0:T(128)} %strength_ref.1, f32[8]{0:T(128)} %omega_ref.1, s32[4]{0:T(128)} %depth_ref.1, ...), custom_call_target="tpu_custom_call" | custom-call | tf_op jit(solution)/shard_map/pallas_call | solution.py:418
  49.7 2.0 %shard_map.130 = (f32[3,4,256,128]{3,2,1,0:T(8,128)}, f32[3,4,256,128]{3,2,1,0:T(8,128)}, f32[2,4,8,4,4,256]{5,4,3,2,1,0:T(4,128)}, f32[2,4,8]{2,1,0:T(4,128)}) custom-call(f32[3,4,264,128]{3,2,1,0:T(8,128)S(1)} %get-tuple-element.8.eb, f32[3,4,264,128]{3,2,1,0:T(8,128)S(1)} %get-tuple-element.9.hb, f32[2,4,8,4,4,256]{5,4,3,2,1,0:T(4,128)S(1)} %get-tuple-element.10.mon, ...), custom_call_target="tpu_custom_call" | custom-call | tf_op jit(solution)/shard_map/pallas_call | solution.py:458
